TPU v7x, 512 devices: a whole 4x4x16 slice. The times are simulated.
512 devices in a mesh: space: 64 (over z, x), member: 8 (over y, core).
Axes of the slice: x: 4, y: 4, z: 16, core: 2. Of those that a mesh axis runs over, the one named last changes fastest.
Arguments:
- spectra: float32 [16, 36, 256, 720], P('member', None, 'space'), may hold values from 0.5 to 2
- group_speed: float32 [256, 720], P('space'), may hold values from 0.15 to 0.5
- turning_rate: float32 [256, 720], P('space'), may hold values from -0.28 to 0.28
- obs_cell: int32 [2, 1024], replicated, may hold values from 0 to 184319, as said below
- obs_value: float32 [2, 1024], replicated, may hold values from 0.9 to 1.6
- obs_variance: float32 [2, 1024], replicated, may hold values from 0.001 to 0.01
Outputs:
- analysis: float32 [16, 36, 184320], P(None, None, ('space', 'member'))
Inputs may be any that keep to these rules, and one draw needn't show every extreme that they name: `obs_cell`: every block of 360 consecutive cells starting at a multiple of 360 holds the cell of at least one observation in every batch.
All inputs are finite; a program needn't handle non-finite values.
Results may differ from a plain program's by a relative error of at most 0.0003.
Values sent between devices are 32-bit elements; how exact they have to be, the bound alone decides.
A program may use at most 64 MiB of HBM per device.

v0:
```python
import math

import jax
import jax.numpy as jnp
from jax import lax
from jax.sharding import PartitionSpec as P

LON = 720
STEPS = 4
BATCHES = 2
LOC = 4


HIGH = lax.Precision.HIGHEST


def padded_2(cells, sides, width):
    for axis, dim in sides:
        count = lax.axis_size(axis)
        ends = count - 1
        head = lax.slice_in_dim(cells, 0, width, axis=dim)
        tail = lax.slice_in_dim(cells, cells.shape[dim] - width, cells.shape[dim], axis=dim)
        cells = jnp.concatenate(
            [
                lax.ppermute(tail, axis, [(i, (i + 1) % count) for i in range(ends)]),
                cells,
                lax.ppermute(head, axis, [((i + 1) % count, i) for i in range(ends)]),
            ],
            axis=dim,
        )
    return cells


def copy_for_each(array, axis):
    devices = lax.axis_size(axis)
    return lax.all_to_all(
        jnp.broadcast_to(array[None], (devices, *array.shape)), axis, 0, 0, tiled=True
    )


def over_copies(array, axis):
    everything = copy_for_each(array, axis)
    return jnp.sum(everything, axis=0)


def transport(padded, speed, turning, cosines, sines):
    centre = padded[:, :, 1:-1, :]
    south = padded[:, :, :-2, :]
    north = padded[:, :, 2:, :]
    along_x = speed[None] * cosines[:, None, None]
    along_y = speed[None] * sines[:, None, None]
    along_turn = turning[None] * cosines[:, None, None]
    west = jnp.roll(centre, 1, axis=3)
    east = jnp.roll(centre, -1, axis=3)
    behind = jnp.roll(centre, 1, axis=1)
    ahead = jnp.roll(centre, -1, axis=1)
    result = (
        centre
        - jnp.maximum(along_x, 0.0) * (centre - west)
        - jnp.minimum(along_x, 0.0) * (east - centre)
    )
    result = (
        result
        - jnp.maximum(along_y, 0.0) * (centre - south)
        - jnp.minimum(along_y, 0.0) * (north - centre)
    )
    result = (
        result
        - jnp.maximum(along_turn, 0.0) * (centre - behind)
        - jnp.minimum(along_turn, 0.0) * (ahead - centre)
    )
    return result


def panel(prior, values, variance):
    members = prior.shape[1]
    centre = jnp.mean(prior, axis=1)
    anomaly = prior - centre[:, None]
    spread = jnp.sum(anomaly * anomaly, axis=1) / (members - 1)
    total = spread + variance
    shrink = 1.0 / (1.0 + jnp.sqrt(variance / total))
    weights_obs = ((values - centre)[:, None] - shrink[:, None] * anomaly) / total[:, None]
    outer = anomaly[:, :, None] * weights_obs[:, None, :]
    return outer.reshape(prior.shape[0], members * members) / (members - 1)


def taper(cell_ids, targets):
    lat_gap = cell_ids[:, None] // LON - targets[None, :] // LON
    lon_gap = jnp.abs(cell_ids[:, None] % LON - targets[None, :] % LON)
    lon_gap = jnp.minimum(lon_gap, LON - lon_gap)
    square = (lat_gap * lat_gap + lon_gap * lon_gap).astype(jnp.float32)
    near = jnp.maximum(1.0 - square / (LOC * LOC), 0.0)
    return near * near


def per_device(spectra, group_speed, turning_rate, obs_cell, obs_value, obs_variance):
    local_members, directions, rows, width = spectra.shape
    angles = 2.0 * math.pi * jnp.arange(directions, dtype=jnp.float32) / directions
    cosines = jnp.cos(angles)
    sines = jnp.sin(angles)
    energy = spectra
    for step in range(STEPS):
        padded = padded_2(energy, (("space", 2),), 1)
        energy = transport(padded, group_speed, turning_rate, cosines, sines)
    state = lax.all_to_all(
        energy.reshape(local_members, directions, rows * width),
        "member",
        split_axis=2,
        concat_axis=0,
        tiled=True,
    )
    members, directions, owned = state.shape
    first_cell = (
        lax.axis_index("space") * lax.axis_size("member") + lax.axis_index("member")
    ) * owned
    cell_ids = first_cell + jnp.arange(owned, dtype=jnp.int32)
    for batch in range(BATCHES):
        targets = obs_cell[batch]
        mean_dir = jnp.mean(state, axis=1)
        onehot = (targets[:, None] == cell_ids[None, :]).astype(jnp.float32)
        partial_prior = jnp.dot(onehot, mean_dir.T, precision=HIGH)
        slab_prior = over_copies(partial_prior, "member")
        beside_all = padded_2(slab_prior[None], (("space", 0),), 1)
        prior = jnp.sum(beside_all, axis=0)
        mixing = panel(prior, obs_value[batch], obs_variance[batch])
        gain = jnp.dot(taper(cell_ids, targets), mixing, precision=HIGH).reshape(
            owned, members, members
        )
        deviation = state - jnp.mean(state, axis=0, keepdims=True)
        state = state + jnp.einsum("kdc,ckl->ldc", deviation, gain, precision=HIGH)
    return state


def solution(mesh):
    placed = (P("member", None, "space", None), P("space", None), P("space", None), P(), P(), P())
    return jax.shard_map(
        per_device,
        mesh=mesh,
        in_specs=placed,
        out_specs=P(None, None, ("space", "member")),
        check_vma=False,
    )
```

profile of v0, /device:TPU:102, one launch (start us, length us, event | category | flops | bytes accessed | tf_op | source)
XLA Modules:
  0.0 194.1 jit_solution(2479666879118172591)
XLA Ops:
  1.4 5.0 %collective-permute-start = (f32[2,36,1,720]{3,1,2,0:T(8,128)S(1)}, f32[2,36,1,720]{3,1,2,0:T(8,128)S(1)}, u32[]{:S(2)}, u32[]{:S(2)}) collective-permute-start(f32[2,36,1,720]{3,1,2,0:T(8,128)S(1)} %get-tuple-element.51), channel_id=1, source_target_pairs={{0,8},{8,16},{16,24},{24,32},{32,40},{40,48},{48,56},{56,64},{64,7... | collective-permute-start | bytes 622088 | tf_op jit(solution)/shard_map/ppermute | solution.py:25
  11.5 7.4 %collective-permute-done.1 = f32[2,36,1,720]{3,1,2,0:T(8,128)S(1)} collective-permute-done((f32[2,36,1,720]{3,1,2,0:T(8,128)S(1)}, f32[2,36,1,720]{3,1,2,0:T(8,128)S(1)}, u32[]{:S(2)}, u32[]{:S(2)}) %collective-permute-start.1) | collective-permute-done | bytes 207392 | tf_op jit(solution)/shard_map/ppermute | solution.py:27
  22.5 3.9 %collective-permute-start.3 = (f32[2,36,1,720]{3,1,2,0:T(8,128)S(1)}, f32[2,36,1,720]{3,1,2,0:T(8,128)S(1)}, u32[]{:S(2)}, u32[]{:S(2)}) collective-permute-start(f32[2,36,1,720]{3,1,2,0:T(8,128)S(1)} %get-tuple-element.42), channel_id=1, source_target_pairs={{8,0},{16,8},{24,16},{32,24},{40,32},{48,40},{56,48},{64,56},{72,6... | collective-permute-start | bytes 622088 | tf_op jit(solution)/shard_map/ppermute | solution.py:27
  26.4 2.5 %collective-permute-done.2 = f32[2,36,1,720]{3,1,2,0:T(8,128)S(1)} collective-permute-done((f32[2,36,1,720]{3,1,2,0:T(8,128)S(1)}, f32[2,36,1,720]{3,1,2,0:T(8,128)S(1)}, u32[]{:S(2)}, u32[]{:S(2)}) %collective-permute-start.2) | collective-permute-done | bytes 207392 | tf_op jit(solution)/shard_map/ppermute | solution.py:25
  28.9 5.2 %collective-permute-done.3 = f32[2,36,1,720]{3,1,2,0:T(8,128)S(1)} collective-permute-done((f32[2,36,1,720]{3,1,2,0:T(8,128)S(1)}, f32[2,36,1,720]{3,1,2,0:T(8,128)S(1)}, u32[]{:S(2)}, u32[]{:S(2)}) %collective-permute-start.3) | collective-permute-done | bytes 207392 | tf_op jit(solution)/shard_map/ppermute | solution.py:27
  37.7 3.9 %collective-permute-start.5 = (f32[2,36,1,720]{3,1,2,0:T(8,128)S(1)}, f32[2,36,1,720]{3,1,2,0:T(8,128)S(1)}, u32[]{:S(2)}, u32[]{:S(2)}) collective-permute-start(f32[2,36,1,720]{3,1,2,0:T(8,128)S(1)} %get-tuple-element.32), channel_id=1, source_target_pairs={{8,0},{16,8},{24,16},{32,24},{40,32},{48,40},{56,48},{64,56},{72,6... | collective-permute-start | bytes 622088 | tf_op jit(solution)/shard_map/ppermute | solution.py:27
  41.6 2.2 %collective-permute-done.4 = f32[2,36,1,720]{3,1,2,0:T(8,128)S(1)} collective-permute-done((f32[2,36,1,720]{3,1,2,0:T(8,128)S(1)}, f32[2,36,1,720]{3,1,2,0:T(8,128)S(1)}, u32[]{:S(2)}, u32[]{:S(2)}) %collective-permute-start.4) | collective-permute-done | bytes 207392 | tf_op jit(solution)/shard_map/ppermute | solution.py:25
  43.8 5.2 %collective-permute-done.5 = f32[2,36,1,720]{3,1,2,0:T(8,128)S(1)} collective-permute-done((f32[2,36,1,720]{3,1,2,0:T(8,128)S(1)}, f32[2,36,1,720]{3,1,2,0:T(8,128)S(1)}, u32[]{:S(2)}, u32[]{:S(2)}) %collective-permute-start.5) | collective-permute-done | bytes 207392 | tf_op jit(solution)/shard_map/ppermute | solution.py:27
  52.6 3.9 %collective-permute-start.7 = (f32[2,36,1,720]{3,1,2,0:T(8,128)S(1)}, f32[2,36,1,720]{3,1,2,0:T(8,128)S(1)}, u32[]{:S(2)}, u32[]{:S(2)}) collective-permute-start(f32[2,36,1,720]{3,1,2,0:T(8,128)S(1)} %get-tuple-element.22), channel_id=1, source_target_pairs={{8,0},{16,8},{24,16},{32,24},{40,32},{48,40},{56,48},{64,56},{72,6... | collective-permute-start | bytes 622088 | tf_op jit(solution)/shard_map/ppermute | solution.py:27
  58.7 5.2 %collective-permute-done.7 = f32[2,36,1,720]{3,1,2,0:T(8,128)S(1)} collective-permute-done((f32[2,36,1,720]{3,1,2,0:T(8,128)S(1)}, f32[2,36,1,720]{3,1,2,0:T(8,128)S(1)}, u32[]{:S(2)}, u32[]{:S(2)}) %collective-permute-start.7) | collective-permute-done | bytes 207392 | tf_op jit(solution)/shard_map/ppermute | solution.py:27
  65.9 4.6 %copy.102 = f32[2,36,4,720]{1,0,3,2:T(2,128)S(1)} copy(f32[2,36,4,720]{3,1,2,0:T(8,128)} %fusion.52) | data formatting | bytes 1658880 | tf_op jit(solution)/shard_map/reshape | solution.py:106
  70.5 6.2 %reshape.338 = f32[8,1,25920]{2,1,0:T(1,128)} reshape(f32[2880,2,36]{2,1,0:T(2,128)S(1)} %bitcast.80) | data formatting | bytes 1658880
  76.8 4.6 %all-to-all-start = ((f32[8,1,25920]{2,1,0:T(1,128)}), f32[8,1,25920]{2,1,0:T(1,128)S(1)}, u32[]{:S(2)}, u32[]{:S(2)}) async-start(f32[8,1,25920]{2,1,0:T(1,128)} %reshape.338), calls=%async_computation | async-start | bytes 1662976 | tf_op jit(solution)/shard_map/all_to_all | solution.py:105
  81.5 13.5 %all-to-all-done = f32[8,1,25920]{2,1,0:T(1,128)S(1)} async-done(((f32[8,1,25920]{2,1,0:T(1,128)}), f32[8,1,25920]{2,1,0:T(1,128)S(1)}, u32[]{:S(2)}, u32[]{:S(2)}) %all-to-all-start) | async-done | bytes 829472 | tf_op jit(solution)/shard_map/all_to_all | solution.py:105
  95.6 3.7 %reduce.8 = f32[8,25920]{1,0:T(8,128)} reduce(f32[8,1,25920]{2,1,0:T(1,128)S(1)} %all-to-all-done, f32[]{:T(128)} %broadcast.417), dimensions={1}, to_apply=%all_to_all.19.reduce_sub_computation | reduce | bytes 1658884 | tf_op jit(solution)/shard_map/all_to_all | solution.py:105
  99.4 6.2 %reshape.339 = f32[2880,2,36]{2,1,0:T(2,128)S(1)} reshape(f32[8,25920]{1,0:T(8,128)} %reduce.8) | data formatting | bytes 1658880
  105.5 3.0 %copy.103 = f32[2,36,8,360]{3,2,0,1:T(8,128)} copy(f32[2,36,8,360]{1,0,3,2:T(2,128)S(1)} %bitcast.81) | data formatting | bytes 1658880 | tf_op jit(solution)/shard_map/all_to_all | solution.py:105
  111.7 3.5 %all-to-all-start.1 = ((f32[8,1024,16]{1,2,0:T(8,128)}), f32[8,1024,16]{1,2,0:T(8,128)S(1)}, u32[]{:S(2)}, u32[]{:S(2)}) async-start(f32[8,1024,16]{1,2,0:T(8,128)} %broadcast_in_dim.8), calls=%async_computation.1 | async-start | bytes 1048576 | tf_op jit(solution)/shard_map/all_to_all | solution.py:36
  115.3 10.2 %all-to-all-done.1 = f32[8,1024,16]{1,2,0:T(8,128)S(1)} async-done(((f32[8,1024,16]{1,2,0:T(8,128)}), f32[8,1024,16]{1,2,0:T(8,128)S(1)}, u32[]{:S(2)}, u32[]{:S(2)}) %all-to-all-start.1) | async-done | bytes 524320 | tf_op jit(solution)/shard_map/all_to_all | solution.py:36
  127.5 4.1 %collective-permute-start.9 = (f32[1,1024,16]{1,2,0:T(8,128)S(1)}, f32[1,1024,16]{1,2,0:T(8,128)S(1)}, u32[]{:S(2)}, u32[]{:S(2)}) collective-permute-start(f32[1,1024,16]{1,2,0:T(8,128)S(1)} %bitcast.84), channel_id=1, source_target_pairs={{8,0},{16,8},{24,16},{32,24},{40,32},{48,40},{56,48},{64,56},{72,6... | collective-permute-start | bytes 196616 | tf_op jit(solution)/shard_map/ppermute | solution.py:27
  131.6 2.9 %copy.94 = f32[8,2,36,360]{2,1,0,3:T(2,128)} copy(f32[8,2,36,360]{3,0,1,2:T(8,128)S(1)} %bitcast.82) | data formatting | bytes 1658880 | tf_op jit(solution)/shard_map/all_to_all | solution.py:105
  134.7 2.3 %collective-permute-done.9 = f32[1,1024,16]{1,2,0:T(8,128)S(1)} collective-permute-done((f32[1,1024,16]{1,2,0:T(8,128)S(1)}, f32[1,1024,16]{1,2,0:T(8,128)S(1)}, u32[]{:S(2)}, u32[]{:S(2)}) %collective-permute-start.9) | collective-permute-done | bytes 65568 | tf_op jit(solution)/shard_map/ppermute | solution.py:27
  137.1 2.8 %fusion.20 = f32[360,16,16]{0,2,1:T(8,128)S(1)} fusion(s32[1024]{0:T(1024)S(1)} %bitcast.94, s32[360]{0:T(512)S(1)} %get-tuple-element.84, s32[1024]{0:T(1024)S(1)} %bitcast.95, s32[360]{0:T(512)S(1)} %get-tuple-element.85, f32[1024,16]{0,1:T(8,128)S(1)} %subtract_divide_fusion.1, f32[1024,16]{0,1:T(8,128)S(1)} %get-tuple-element.12), kind=kOutput, calls=%fused_computation.20 | convolution fusion | flops 1137778688 | bytes 510784 | tf_op jit(solution)/shard_map/dot_general | solution.py:126
  142.0 8.5 %fusion.154 = (f32[36,360]{0,1:T(8,128)}, f32[16,360]{0,1:T(8,128)S(1)}, f32[16,36,360]{1,0,2:T(8,128)S(1)}) fusion(f32[16,36,360]{1,0,2:T(8,128)} %bitcast.79, f32[360,16,16]{1,2,0:T(8,128)} %copy.97, f32[36,360]{0,1:T(8,128)S(1)} %copy.96), kind=kOutput, calls=%fused_computation.212 | convolution fusion | flops 40623840 | bytes 2154240 | tf_op jit(solution)/shard_map/kdc,ckl->ldc/dot_general | solution.py:130
  152.3 3.5 %all-to-all-start.2 = ((f32[8,1024,16]{1,2,0:T(8,128)}), f32[8,1024,16]{1,2,0:T(8,128)S(1)}, u32[]{:S(2)}, u32[]{:S(2)}) async-start(f32[8,1024,16]{1,2,0:T(8,128)} %broadcast_in_dim.10), calls=%async_computation.2 | async-start | bytes 1048576 | tf_op jit(solution)/shard_map/all_to_all | solution.py:36
  157.4 8.6 %all-to-all-done.2 = f32[8,1024,16]{1,2,0:T(8,128)S(1)} async-done(((f32[8,1024,16]{1,2,0:T(8,128)}), f32[8,1024,16]{1,2,0:T(8,128)S(1)}, u32[]{:S(2)}, u32[]{:S(2)}) %all-to-all-start.2) | async-done | bytes 524320 | tf_op jit(solution)/shard_map/all_to_all | solution.py:36
  166.1 3.0 %collective-permute-start.10 = (f32[1,1024,16]{1,2,0:T(8,128)S(1)}, f32[1,1024,16]{1,2,0:T(8,128)S(1)}, u32[]{:S(2)}, u32[]{:S(2)}) collective-permute-start(f32[1,1024,16]{1,2,0:T(8,128)S(1)} %bitcast.85), channel_id=1, source_target_pairs={{0,8},{8,16},{16,24},{24,32},{32,40},{40,48},{48,56},{56,64},{64,7... | collective-permute-start | bytes 196616 | tf_op jit(solution)/shard_map/ppermute | solution.py:25
  169.1 3.1 %collective-permute-start.11 = (f32[1,1024,16]{1,2,0:T(8,128)S(1)}, f32[1,1024,16]{1,2,0:T(8,128)S(1)}, u32[]{:S(2)}, u32[]{:S(2)}) collective-permute-start(f32[1,1024,16]{1,2,0:T(8,128)S(1)} %bitcast.86), channel_id=1, source_target_pairs={{8,0},{16,8},{24,16},{32,24},{40,32},{48,40},{56,48},{64,56},{72,6... | collective-permute-start | bytes 196616 | tf_op jit(solution)/shard_map/ppermute | solution.py:27
  173.2 5.4 %collective-permute-done.11 = f32[1,1024,16]{1,2,0:T(8,128)S(1)} collective-permute-done((f32[1,1024,16]{1,2,0:T(8,128)S(1)}, f32[1,1024,16]{1,2,0:T(8,128)S(1)}, u32[]{:S(2)}, u32[]{:S(2)}) %collective-permute-start.11) | collective-permute-done | bytes 65568 | tf_op jit(solution)/shard_map/ppermute | solution.py:27
  178.7 3.5 %fusion.30 = f32[360,16,16]{0,2,1:T(8,128)S(1)} fusion(s32[1024]{0:T(1024)S(1)} %bitcast.91, s32[1024]{0:T(1024)S(1)} %bitcast.92, s32[360]{0:T(512)} %copy-done.6, s32[360]{0:T(512)} %copy-done.7, f32[1024,16]{0,1:T(8,128)S(1)} %subtract_divide_fusion, f32[1024,16]{0,1:T(8,128)S(1)} %get-tuple-element.10), kind=kOutput, calls=%fused_computation.29 | convolution fusion | flops 1137778688 | bytes 510784 | tf_op jit(solution)/shard_map/dot_general | solution.py:126
  184.3 6.7 %bitcast_add_fusion = f32[16,36,360]{1,0,2:T(8,128)} fusion(f32[16,36,360]{1,0,2:T(8,128)S(1)} %get-tuple-element.81, f32[360,16,16]{1,2,0:T(8,128)} %copy.100, f32[36,360]{0,1:T(8,128)S(1)} %copy.99), kind=kOutput, calls=%fused_computation | convolution fusion | flops 40227840 | bytes 2079360 | tf_op jit(solution)/shard_map/kdc,ckl->ldc/dot_general | solution.py:130
  190.9 3.1 %copy.101 = f32[16,36,360]{2,0,1:T(8,128)} copy(f32[16,36,360]{1,0,2:T(8,128)} %bitcast_add_fusion) | data formatting | bytes 1658880 | tf_op jit(solution)/shard_map/add | solution.py:130
  (85 shorter events, 35.9 us)
Async XLA Ops:
  1.4 10.2 %collective-permute-start = (f32[2,36,1,720]{3,1,2,0:T(8,128)S(1)}, f32[2,36,1,720]{3,1,2,0:T(8,128)S(1)}, u32[]{:S(2)}, u32[]{:S(2)}) collective-permute-start(f32[2,36,1,720]{3,1,2,0:T(8,128)S(1)} %get-tuple-element.51), channel_id=1, source_target_pairs={{0,8},{8,16},{16,24},{24,32},{32,40},{40,48},{48,56},{56,64},{64,7... | collective-permute-start | bytes 622088 | tf_op jit(solution)/shard_map/ppermute | solution.py:25
  6.3 12.6 %collective-permute-start.1 = (f32[2,36,1,720]{3,1,2,0:T(8,128)S(1)}, f32[2,36,1,720]{3,1,2,0:T(8,128)S(1)}, u32[]{:S(2)}, u32[]{:S(2)}) collective-permute-start(f32[2,36,1,720]{3,1,2,0:T(8,128)S(1)} %get-tuple-element.52), channel_id=1, source_target_pairs={{8,0},{16,8},{24,16},{32,24},{40,32},{48,40},{56,48},{64,56},{72,6... | collective-permute-start | bytes 622088 | tf_op jit(solution)/shard_map/ppermute | solution.py:27
  8.5 0.7 copy-start.1
  8.5 0.7 copy-start.2
  20.5 8.4 %collective-permute-start.2 = (f32[2,36,1,720]{3,1,2,0:T(8,128)S(1)}, f32[2,36,1,720]{3,1,2,0:T(8,128)S(1)}, u32[]{:S(2)}, u32[]{:S(2)}) collective-permute-start(f32[2,36,1,720]{3,1,2,0:T(8,128)S(1)} %get-tuple-element.41), channel_id=1, source_target_pairs={{0,8},{8,16},{16,24},{24,32},{32,40},{40,48},{48,56},{56,64},{64,7... | collective-permute-start | bytes 622088 | tf_op jit(solution)/shard_map/ppermute | solution.py:25
  22.5 11.7 %collective-permute-start.3 = (f32[2,36,1,720]{3,1,2,0:T(8,128)S(1)}, f32[2,36,1,720]{3,1,2,0:T(8,128)S(1)}, u32[]{:S(2)}, u32[]{:S(2)}) collective-permute-start(f32[2,36,1,720]{3,1,2,0:T(8,128)S(1)} %get-tuple-element.42), channel_id=1, source_target_pairs={{8,0},{16,8},{24,16},{32,24},{40,32},{48,40},{56,48},{64,56},{72,6... | collective-permute-start | bytes 622088 | tf_op jit(solution)/shard_map/ppermute | solution.py:27
  35.7 8.1 %collective-permute-start.4 = (f32[2,36,1,720]{3,1,2,0:T(8,128)S(1)}, f32[2,36,1,720]{3,1,2,0:T(8,128)S(1)}, u32[]{:S(2)}, u32[]{:S(2)}) collective-permute-start(f32[2,36,1,720]{3,1,2,0:T(8,128)S(1)} %get-tuple-element.31), channel_id=1, source_target_pairs={{0,8},{8,16},{16,24},{24,32},{32,40},{40,48},{48,56},{56,64},{64,7... | collective-permute-start | bytes 622088 | tf_op jit(solution)/shard_map/ppermute | solution.py:25
  37.7 11.4 %collective-permute-start.5 = (f32[2,36,1,720]{3,1,2,0:T(8,128)S(1)}, f32[2,36,1,720]{3,1,2,0:T(8,128)S(1)}, u32[]{:S(2)}, u32[]{:S(2)}) collective-permute-start(f32[2,36,1,720]{3,1,2,0:T(8,128)S(1)} %get-tuple-element.32), channel_id=1, source_target_pairs={{8,0},{16,8},{24,16},{32,24},{40,32},{48,40},{56,48},{64,56},{72,6... | collective-permute-start | bytes 622088 | tf_op jit(solution)/shard_map/ppermute | solution.py:27
  50.6 8.1 %collective-permute-start.6 = (f32[2,36,1,720]{3,1,2,0:T(8,128)S(1)}, f32[2,36,1,720]{3,1,2,0:T(8,128)S(1)}, u32[]{:S(2)}, u32[]{:S(2)}) collective-permute-start(f32[2,36,1,720]{3,1,2,0:T(8,128)S(1)} %get-tuple-element.21), channel_id=1, source_target_pairs={{0,8},{8,16},{16,24},{24,32},{32,40},{40,48},{48,56},{56,64},{64,7... | collective-permute-start | bytes 622088 | tf_op jit(solution)/shard_map/ppermute | solution.py:25
  52.6 11.4 %collective-permute-start.7 = (f32[2,36,1,720]{3,1,2,0:T(8,128)S(1)}, f32[2,36,1,720]{3,1,2,0:T(8,128)S(1)}, u32[]{:S(2)}, u32[]{:S(2)}) collective-permute-start(f32[2,36,1,720]{3,1,2,0:T(8,128)S(1)} %get-tuple-element.22), channel_id=1, source_target_pairs={{8,0},{16,8},{24,16},{32,24},{40,32},{48,40},{56,48},{64,56},{72,6... | collective-permute-start | bytes 622088 | tf_op jit(solution)/shard_map/ppermute | solution.py:27
  76.8 4.6 %copy-start.5 = (s32[2,1024]{1,0:T(2,128)S(1)}, s32[2,1024]{1,0:T(2,128)}, u32[]{:S(2)}) copy-start(s32[2,1024]{1,0:T(2,128)} %param.9) | copy-start | bytes 24580
  76.8 18.2 %all-to-all-start = ((f32[8,1,25920]{2,1,0:T(1,128)}), f32[8,1,25920]{2,1,0:T(1,128)S(1)}, u32[]{:S(2)}, u32[]{:S(2)}) async-start(f32[8,1,25920]{2,1,0:T(1,128)} %reshape.338), calls=%async_computation | async-start | bytes 1662976 | tf_op jit(solution)/shard_map/all_to_all | solution.py:105
  108.6 6.7 %copy-start.3 = (f32[2,1024]{1,0:T(2,128)S(1)}, f32[2,1024]{1,0:T(2,128)}, u32[]{:S(2)}) copy-start(f32[2,1024]{1,0:T(2,128)} %param.10) | copy-start | bytes 24580
  108.6 6.7 %copy-start.4 = (f32[2,1024]{1,0:T(2,128)S(1)}, f32[2,1024]{1,0:T(2,128)}, u32[]{:S(2)}) copy-start(f32[2,1024]{1,0:T(2,128)} %param.11) | copy-start | bytes 24580
  110.0 21.7 %copy-start = (f32[2,36,8,360]{3,2,0,1:T(8,128)S(1)}, f32[2,36,8,360]{3,2,0,1:T(8,128)}, u32[]{:S(2)}) copy-start(f32[2,36,8,360]{3,2,0,1:T(8,128)} %copy.103) | copy-start | bytes 2488324
  111.7 13.8 %all-to-all-start.1 = ((f32[8,1024,16]{1,2,0:T(8,128)}), f32[8,1024,16]{1,2,0:T(8,128)S(1)}, u32[]{:S(2)}, u32[]{:S(2)}) async-start(f32[8,1024,16]{1,2,0:T(8,128)} %broadcast_in_dim.8), calls=%async_computation.1 | async-start | bytes 1048576 | tf_op jit(solution)/shard_map/all_to_all | solution.py:36
  115.3 21.8 %copy-start.6 = (s32[360]{0:T(512)}, s32[360]{0:T(512)S(1)}, u32[]{:S(2)}) copy-start(s32[360]{0:T(512)S(1)} %get-tuple-element.84) | copy-start | bytes 4324
  115.3 21.8 %copy-start.7 = (s32[360]{0:T(512)}, s32[360]{0:T(512)S(1)}, u32[]{:S(2)}) copy-start(s32[360]{0:T(512)S(1)} %get-tuple-element.85) | copy-start | bytes 4324
  125.5 9.1 %collective-permute-start.8 = (f32[1,1024,16]{1,2,0:T(8,128)S(1)}, f32[1,1024,16]{1,2,0:T(8,128)S(1)}, u32[]{:S(2)}, u32[]{:S(2)}) collective-permute-start(f32[1,1024,16]{1,2,0:T(8,128)S(1)} %bitcast.83), channel_id=1, source_target_pairs={{0,8},{8,16},{16,24},{24,32},{32,40},{40,48},{48,56},{56,64},{64,7... | collective-permute-start | bytes 196616 | tf_op jit(solution)/shard_map/ppermute | solution.py:25
  127.5 9.5 %collective-permute-start.9 = (f32[1,1024,16]{1,2,0:T(8,128)S(1)}, f32[1,1024,16]{1,2,0:T(8,128)S(1)}, u32[]{:S(2)}, u32[]{:S(2)}) collective-permute-start(f32[1,1024,16]{1,2,0:T(8,128)S(1)} %bitcast.84), channel_id=1, source_target_pairs={{8,0},{16,8},{24,16},{32,24},{40,32},{48,40},{56,48},{64,56},{72,6... | collective-permute-start | bytes 196616 | tf_op jit(solution)/shard_map/ppermute | solution.py:27
  152.3 13.8 %all-to-all-start.2 = ((f32[8,1024,16]{1,2,0:T(8,128)}), f32[8,1024,16]{1,2,0:T(8,128)S(1)}, u32[]{:S(2)}, u32[]{:S(2)}) async-start(f32[8,1024,16]{1,2,0:T(8,128)} %broadcast_in_dim.10), calls=%async_computation.2 | async-start | bytes 1048576 | tf_op jit(solution)/shard_map/all_to_all | solution.py:36
  166.1 7.1 %collective-permute-start.10 = (f32[1,1024,16]{1,2,0:T(8,128)S(1)}, f32[1,1024,16]{1,2,0:T(8,128)S(1)}, u32[]{:S(2)}, u32[]{:S(2)}) collective-permute-start(f32[1,1024,16]{1,2,0:T(8,128)S(1)} %bitcast.85), channel_id=1, source_target_pairs={{0,8},{8,16},{16,24},{24,32},{32,40},{40,48},{48,56},{56,64},{64,7... | collective-permute-start | bytes 196616 | tf_op jit(solution)/shard_map/ppermute | solution.py:25
  169.1 9.5 %collective-permute-start.11 = (f32[1,1024,16]{1,2,0:T(8,128)S(1)}, f32[1,1024,16]{1,2,0:T(8,128)S(1)}, u32[]{:S(2)}, u32[]{:S(2)}) collective-permute-start(f32[1,1024,16]{1,2,0:T(8,128)S(1)} %bitcast.86), channel_id=1, source_target_pairs={{8,0},{16,8},{24,16},{32,24},{40,32},{48,40},{56,48},{64,56},{72,6... | collective-permute-start | bytes 196616 | tf_op jit(solution)/shard_map/ppermute | solution.py:27
where the time goes:
time: 195 us; the launch traced here: 194 us
  waiting for transfers between devices  72 us (37%)
  starting transfers between devices  48.2 us (25%)
  local copies, waits for them, and re-layouts  38.8 us (20%)
  matrix products  23.2 us (12%)
  other arithmetic  11.4 us (6%)
    ppermute x6, waiting for transfers between devices, padded_2(): lax.ppermute(head, axis, [((i + 1) % count, i) for i in range(ends)])  30.8 us
    ppermute x6, starting transfers between devices, padded_2(): lax.ppermute(head, axis, [((i + 1) % count, i) for i in range(ends)])  21 us
    all_to_all x2, waiting for transfers between devices, copy_for_each(): lax.all_to_all(jnp.broadcast_to(array[None], (devices, *array.shape)), ax...  18.8 us
    ppermute x6, starting transfers between devices, padded_2(): lax.ppermute(tail, axis, [(i, (i + 1) % count) for i in range(ends)])  15.6 us
    dot_general x2, matrix products, per_device(): state = state + jnp.einsum('kdc,ckl->ldc', deviation, gain, precision=HIGH)  15.1 us
    unnamed x19, local copies, waits for them, and re-layouts  14.1 us
    all_to_all x1, waiting for transfers between devices, per_device(): lax.all_to_all(energy.reshape(local_members, directions, rows * width), '...  13.5 us
    ppermute x6, waiting for transfers between devices, padded_2(): lax.ppermute(tail, axis, [(i, (i + 1) % count) for i in range(ends)])  8.82 us
  transfers between devices with their start and end apart: 15, of which 13 were waited for; matrix products, arithmetic and copies ran while one was open for 4% of the time, Pallas kernels for 0%

commit v1 on v0

v1 whole, which is shorter than its diff:
```python
import functools
import math

import jax
import jax.numpy as jnp
from jax import lax
from jax.experimental import pallas as pl
from jax.experimental.pallas import tpu as pltpu
from jax.sharding import PartitionSpec as P

LON = 720
STEPS = 4
BATCHES = 2
LOC = 4
DIRS = 36
NOBS = 1024
MEMBERS = 16
ROWS = 4
OWN = 360
WIDE = 768
TALL = 48
BASE = 8
PART = 384
HALF = 24
CHUNK = 512
F32 = jnp.float32
BF16 = jnp.bfloat16


def step_row(centre, behind, ahead, upwind_y, cx, cy, cr, pick_x):
    west = pltpu.roll(centre, 1, axis=1)
    east = pltpu.roll(centre, WIDE - 1, axis=1)
    result = centre - cx * (centre - jnp.where(pick_x, west, east))
    result = result - cy * (centre - upwind_y)
    return result - jnp.abs(cr) * (centre - jnp.where(cr > 0.0, behind, ahead))


def wave_kernel(
    spaces, peers,
    x_ref, speed_ref, turn_ref, trig_ref, obs_ref,
    state_ref, prior_ref,
    e_ref, south_ref, north_ref, cx_ref, cy_ref, cr_ref, send_ref, mean_ref,
    mine_ref, near_ref, sum_ref,
    halo_send, halo_recv, part_send, part_recv, near_send, near_recv,
    all_send, all_recv, own_sem,
):
    space = lax.axis_index("space")
    member = lax.axis_index("member")
    shifts = (1, spaces - 1, 2, spaces - 2)

    barrier = pltpu.get_barrier_semaphore()
    for shift in shifts:
        pl.semaphore_signal(
            barrier, inc=1, device_id=(lax.rem(space + shift, spaces), member),
            device_id_type=pl.DeviceIdType.MESH)
    for offset in range(1, peers):
        pl.semaphore_signal(
            barrier, inc=1, device_id=(space, lax.rem(member + offset, peers)),
            device_id_type=pl.DeviceIdType.MESH)
    pl.semaphore_wait(barrier, len(shifts) + peers - 1)

    def held(step, m, r):
        return x_ref.at[m, r] if step == 0 else e_ref.at[step - 1, m, r]

    def halo(step, m, side):
        if side == 0:
            source = held(step, m, ROWS - 1).at[pl.ds(BASE, HALF)]
            target, to = south_ref.at[step, m], lax.rem(space + 1, spaces)
        else:
            source = held(step, m, 0).at[pl.ds(BASE + 16, HALF)]
            target, to = north_ref.at[step, m], lax.rem(space + spaces - 1, spaces)
        return pltpu.make_async_remote_copy(
            src_ref=source, dst_ref=target,
            send_sem=halo_send.at[step, m, side], recv_sem=halo_recv.at[step, m, side],
            device_id=(to, member), device_id_type=pl.DeviceIdType.MESH)

    for m in range(2):
        for side in range(2):
            halo(0, m, side).start()

    cosines = jnp.concatenate([trig_ref[0]] * (WIDE // 128), axis=1)
    sines = jnp.concatenate([trig_ref[1]] * (WIDE // 128), axis=1)
    for r in range(ROWS):
        speed = speed_ref[r:r + 1, :]
        cx_ref[r] = speed * jnp.abs(cosines)
        cy_ref[r] = speed * jnp.abs(sines)
        cr_ref[r] = turn_ref[r:r + 1, :] * cosines
    pick_x = cosines > 0.0
    pick_y = sines > 0.0
    has_south = (space > 0).astype(F32)
    has_north = (space < spaces - 1).astype(F32)

    def advance(step, m, r):
        centre = held(step, m, r)[BASE:BASE + DIRS, :]
        behind = held(step, m, r)[BASE - 1:BASE - 1 + DIRS, :]
        ahead = held(step, m, r)[BASE + 1:BASE + 1 + DIRS, :]
        if r > 0:
            south = held(step, m, r - 1)[BASE:BASE + DIRS, :]
        if r < ROWS - 1:
            north = held(step, m, r + 1)[BASE:BASE + DIRS, :]
        if r == 0:
            south = jnp.concatenate([south_ref[step, m] * has_south, north[HALF:]], axis=0)
        if r == ROWS - 1:
            north = jnp.concatenate(
                [south[:16], (north_ref[step, m] * has_north)[:DIRS - 16]], axis=0)
        new = step_row(centre, behind, ahead, jnp.where(pick_y, south, north),
                       cx_ref[r], cy_ref[r], cr_ref[r], pick_x)
        e_ref[step, m, r, BASE:BASE + DIRS, :] = new
        e_ref[step, m, r, BASE - 1:BASE, :] = new[DIRS - 1:DIRS]
        e_ref[step, m, r, BASE + DIRS:BASE + DIRS + 1, :] = new[0:1]
        if step == STEPS - 1:
            mean_ref[m * ROWS + r:m * ROWS + r + 1, :] = (
                jnp.sum(new, axis=0, keepdims=True) * (1.0 / DIRS))
            send_ref[2 * r, m * DIRS:(m + 1) * DIRS, :] = new[:, :PART]
            send_ref[2 * r + 1, m * DIRS:(m + 1) * DIRS, :] = pltpu.roll(
                new, WIDE - OWN, axis=1)[:, :PART]

    cuts = ((0, 32), (32, 40))

    def part(m, offset):
        to = lax.rem(member + offset, peers)
        first, rows = cuts[m]
        return pltpu.make_async_remote_copy(
            src_ref=send_ref.at[to, pl.ds(first, rows)],
            dst_ref=state_ref.at[member, pl.ds(first, rows)],
            send_sem=part_send.at[m, offset], recv_sem=part_recv.at[m, offset],
            device_id=(space, to), device_id_type=pl.DeviceIdType.MESH)

    order = (4, 3, 5, 2, 6, 1, 7)
    for step in range(STEPS):
        for m in range(2):
            for r in range(1, ROWS - 1):
                advance(step, m, r)
            halo(step, m, 0).wait_recv()
            advance(step, m, 0)
            if step < STEPS - 1:
                halo(step + 1, m, 1).start()
            halo(step, m, 1).wait_recv()
            advance(step, m, ROWS - 1)
            if step < STEPS - 1:
                halo(step + 1, m, 0).start()
            else:
                for offset in order:
                    part(m, offset).start()
    own = pltpu.make_async_copy(send_ref.at[member], state_ref.at[member], own_sem)
    own.start()

    mean = mean_ref[...]
    high = mean.astype(BF16)
    rest = mean - high.astype(F32)
    middle = rest.astype(BF16)
    low = (rest - middle.astype(F32)).astype(BF16)
    where_lon = lax.broadcasted_iota(jnp.int32, (WIDE, CHUNK), 0).astype(F32)
    slab = (space * ROWS).astype(F32)
    for chunk in range(BATCHES * NOBS // CHUNK):
        batch, part_of = divmod(chunk, NOBS // CHUNK)
        lanes = slice(part_of * CHUNK, (part_of + 1) * CHUNK)
        onehot = jnp.where(where_lon == obs_ref[2 * batch + 1:2 * batch + 2, lanes], 1.0, 0.0)
        onehot = onehot.astype(BF16)
        found = (
            jnp.dot(high, onehot, preferred_element_type=F32)
            + jnp.dot(middle, onehot, preferred_element_type=F32)
            + jnp.dot(low, onehot, preferred_element_type=F32))
        row = obs_ref[2 * batch:2 * batch + 1, lanes] - slab
        for m in range(2):
            value = jnp.zeros((1, CHUNK), F32)
            for r in range(ROWS):
                value = value + jnp.where(row == float(r), found[m * ROWS + r:m * ROWS + r + 1], 0.0)
            mine_ref[m * 4 + chunk:m * 4 + chunk + 1, :] = value

    def near(index):
        return pltpu.make_async_remote_copy(
            src_ref=mine_ref, dst_ref=near_ref.at[index],
            send_sem=near_send.at[index], recv_sem=near_recv.at[index],
            device_id=(lax.rem(space + shifts[index], spaces), member),
            device_id_type=pl.DeviceIdType.MESH)

    for index in range(4):
        near(index).start()
    for index in range(4):
        near(index).wait_recv()
    sum_ref[...] = mine_ref[...] + near_ref[0] + near_ref[1] + near_ref[2] + near_ref[3]
    prior_ref[member] = sum_ref[...]

    def everyone(offset):
        return pltpu.make_async_remote_copy(
            src_ref=sum_ref, dst_ref=prior_ref.at[member],
            send_sem=all_send.at[offset], recv_sem=all_recv.at[offset],
            device_id=(space, lax.rem(member + offset, peers)),
            device_id_type=pl.DeviceIdType.MESH)

    for offset in order:
        everyone(offset).start()
    for step in range(STEPS):
        for m in range(2):
            for side in range(2):
                halo(step, m, side).wait_send()
    own.wait()
    for index in range(4):
        near(index).wait_send()
    for m in range(2):
        for offset in order:
            part(m, offset).wait()
    for offset in order:
        everyone(offset).wait()


def propagate(x, speed, turn, trig, obs, spaces, peers):
    vmem = pl.BlockSpec(memory_space=pltpu.VMEM)
    dma = pltpu.SemaphoreType.DMA
    return pl.pallas_call(
        functools.partial(wave_kernel, spaces, peers),
        out_shape=(
            jax.ShapeDtypeStruct((peers, 2 * DIRS, PART), F32),
            jax.ShapeDtypeStruct((peers, 8, CHUNK), F32),
        ),
        in_specs=[vmem] * 5,
        out_specs=(vmem, vmem),
        scratch_shapes=[
            pltpu.VMEM((STEPS, 2, ROWS, TALL, WIDE), F32),
            pltpu.VMEM((STEPS, 2, HALF, WIDE), F32),
            pltpu.VMEM((STEPS, 2, HALF, WIDE), F32),
            pltpu.VMEM((ROWS, DIRS, WIDE), F32),
            pltpu.VMEM((ROWS, DIRS, WIDE), F32),
            pltpu.VMEM((ROWS, DIRS, WIDE), F32),
            pltpu.VMEM((2 * ROWS, 2 * DIRS, PART), F32),
            pltpu.VMEM((2 * ROWS, WIDE), F32),
            pltpu.VMEM((8, CHUNK), F32),
            pltpu.VMEM((4, 8, CHUNK), F32),
            pltpu.VMEM((8, CHUNK), F32),
            dma((STEPS, 2, 2)), dma((STEPS, 2, 2)),
            dma((2, 8)), dma((2, 8)),
            dma((4,)), dma((4,)),
            dma((8,)), dma((8,)),
            dma(()),
        ],
        compiler_params=pltpu.CompilerParams(collective_id=0, has_side_effects=True),
        name="propagate",
    )(x, speed, turn, trig, obs)


def panel(prior, values, variance):
    centre = jnp.sum(prior, axis=0, keepdims=True) * (1.0 / MEMBERS)
    anomaly = prior - centre
    spread = jnp.sum(anomaly * anomaly, axis=0, keepdims=True) * (1.0 / (MEMBERS - 1))
    total = spread + variance
    shrink = 1.0 / (1.0 + jnp.sqrt(variance / total))
    coef = ((values - centre) - shrink * anomaly) / (total * (MEMBERS - 1))
    return anomaly, coef


def split_mix(anomaly, coef, high_ref, low_ref):
    for l in range(MEMBERS):
        mix = anomaly * coef[l:l + 1]
        high = mix.astype(BF16)
        high_ref[l * MEMBERS:(l + 1) * MEMBERS, :] = high
        low_ref[l * MEMBERS:(l + 1) * MEMBERS, :] = (mix - high.astype(F32)).astype(BF16)


def taper(row, lon, rows, lons):
    lat_gap = row - rows
    lon_gap = jnp.abs(lon - lons)
    lon_gap = jnp.minimum(lon_gap, LON - lon_gap)
    near = jnp.maximum(1.0 - (lat_gap * lat_gap + lon_gap * lon_gap) * (1.0 / (LOC * LOC)), 0.0)
    return (near * near).astype(BF16)


def mixed(high_ref, low_ref, weights):
    dims = (((1,), (1,)), ((), ()))
    return lax.dot_general(
        high_ref[...], weights, dims, preferred_element_type=F32
    ) + lax.dot_general(low_ref[...], weights, dims, preferred_element_type=F32)


def analyse_kernel(
    peers, state_ref, block_ref, obs_ref, out_ref,
    s_ref, d_ref, prior_ref, next_ref, high_ref, low_ref, gain_ref, column_ref,
):
    device = lax.axis_index("space") * peers + lax.axis_index("member")
    own_row = (device // 2).astype(F32)
    own_lon = ((device % 2) * OWN).astype(F32)
    for k in range(MEMBERS):
        first = (k % 2) * DIRS
        s_ref[k] = state_ref[k // 2, first:first + DIRS, :]
        for chunk in range(4):
            at = (k % 2) * 4 + chunk
            prior_ref[k:k + 1, chunk * CHUNK:(chunk + 1) * CHUNK] = block_ref[k // 2, at:at + 1, :]
    column_ref[...] = jnp.transpose(obs_ref[...])

    cell_lon = lax.broadcasted_iota(jnp.int32, (PART, 128), 0).astype(F32) + own_lon
    cell_lon = jnp.concatenate([cell_lon] * (NOBS // 128), axis=1)

    def assimilate(batch, last):
        weights = taper(own_row, cell_lon, obs_ref[2 * batch:2 * batch + 1, :],
                        obs_ref[2 * batch + 1:2 * batch + 2, :])
        gain_ref[...] = mixed(high_ref, low_ref, weights).reshape(MEMBERS, MEMBERS, PART)
        mean = s_ref[0]
        for k in range(1, MEMBERS):
            mean = mean + s_ref[k]
        mean = mean * (1.0 / MEMBERS)
        for k in range(MEMBERS):
            d_ref[k] = s_ref[k] - mean

        def one(l, carry):
            for tile in range(PART // 128):
                lanes = slice(tile * 128, (tile + 1) * 128)
                total = s_ref[l, :, lanes]
                gain = gain_ref[l, :, lanes]
                for k in range(MEMBERS):
                    total = total + d_ref[k, :, lanes] * gain[k:k + 1]
                if last:
                    count = min(128, OWN - tile * 128)
                    out_ref[l, :, tile * 128:tile * 128 + count] = total[:, :count]
                else:
                    s_ref[l, :, lanes] = total
            return carry

        lax.fori_loop(0, MEMBERS, one, 0)

    anomaly, coef = panel(prior_ref[:, :NOBS], obs_ref[4:5, :], obs_ref[6:7, :])
    split_mix(anomaly, coef, high_ref, low_ref)
    width = 256
    for at in range(0, NOBS, width):
        weights = taper(column_ref[at:at + width, 2:3], column_ref[at:at + width, 3:4],
                        obs_ref[0:1, :], obs_ref[1:2, :])
        gain = mixed(high_ref, low_ref, weights)
        prior = prior_ref[:, NOBS + at:NOBS + at + width]
        deviation = prior - jnp.sum(prior, axis=0, keepdims=True) * (1.0 / MEMBERS)
        for l in range(MEMBERS):
            next_ref[l:l + 1, at:at + width] = prior[l:l + 1] + jnp.sum(
                deviation * gain[l * MEMBERS:(l + 1) * MEMBERS], axis=0, keepdims=True)
    assimilate(0, False)
    anomaly, coef = panel(next_ref[...], obs_ref[5:6, :], obs_ref[7:8, :])
    split_mix(anomaly, coef, high_ref, low_ref)
    assimilate(1, True)


def analyse(state, blocks, obs, peers):
    vmem = pl.BlockSpec(memory_space=pltpu.VMEM)
    return pl.pallas_call(
        functools.partial(analyse_kernel, peers),
        out_shape=jax.ShapeDtypeStruct((MEMBERS, DIRS, OWN), F32),
        in_specs=[vmem] * 3,
        out_specs=vmem,
        scratch_shapes=[
            pltpu.VMEM((MEMBERS, DIRS, PART), F32),
            pltpu.VMEM((MEMBERS, DIRS, PART), F32),
            pltpu.VMEM((MEMBERS, BATCHES * NOBS), F32),
            pltpu.VMEM((MEMBERS, NOBS), F32),
            pltpu.VMEM((MEMBERS * MEMBERS, NOBS), BF16),
            pltpu.VMEM((MEMBERS * MEMBERS, NOBS), BF16),
            pltpu.VMEM((MEMBERS, MEMBERS, PART), F32),
            pltpu.VMEM((NOBS, 8), F32),
        ],
        name="analyse",
    )(state, blocks, obs)


def widen(array):
    return jnp.concatenate([array, array[..., :24], array[..., -24:]], axis=-1)


def per_device(spectra, group_speed, turning_rate, obs_cell, obs_value, obs_variance):
    spaces, peers = lax.axis_size("space"), lax.axis_size("member")
    angles = 2.0 * math.pi * jnp.arange(DIRS, dtype=F32) / DIRS
    trig = jnp.broadcast_to(jnp.stack([jnp.cos(angles), jnp.sin(angles)])[:, :, None], (2, DIRS, 128))
    x = jnp.transpose(spectra, (0, 2, 1, 3))
    x = widen(jnp.concatenate([x[:, :, -BASE:], x, x[:, :, :TALL - BASE - DIRS]], axis=2))
    rows = (obs_cell // LON).astype(F32)
    lons = (obs_cell % LON).astype(F32)
    places = jnp.stack([rows, lons], axis=1).reshape(2 * BATCHES, NOBS)
    obs = jnp.concatenate([places, obs_value, obs_variance], axis=0)
    state, blocks = propagate(x, widen(group_speed), widen(turning_rate), trig, obs, spaces, peers)
    return analyse(state, blocks, obs, peers)


def solution(mesh):
    placed = (P("member", None, "space", None), P("space", None), P("space", None), P(), P(), P())
    return jax.shard_map(
        per_device,
        mesh=mesh,
        in_specs=placed,
        out_specs=P(None, None, ("space", "member")),
        check_vma=False,
    )
```

time: 195 us -> 68 us (0.35)
  the two profiles are of different devices: /device:TPU:102 before, /device:TPU:1 now
where the time goes in v1:
time: 68 us; the launch traced here: 67.7 us
  Pallas kernels  60.4 us (89%)
  local copies, waits for them, and re-layouts  4.57 us (7%)
  other arithmetic  2.65 us (4%)
    pallas_call x1, Pallas kernels, propagate(): pl.pallas_call(functools.partial(wave_kernel, spaces, peers), out_shape=(...  50.2 us
    pallas_call x1, Pallas kernels, analyse(): pl.pallas_call(functools.partial(analyse_kernel, peers), out_shape=jax.Sh...  10.2 us
    pallas_call x1, local copies, waits for them, and re-layouts, analyse(): pl.pallas_call(functools.partial(analyse_kernel, peers), out_shape=jax.Sh...  2.28 us
    concatenate x2, other arithmetic, widen(): return jnp.concatenate([array, array[..., :24], array[..., -24:]], axis=-1)  1.92 us
    unnamed x11, local copies, waits for them, and re-layouts  1.37 us

profile of v1, /device:TPU:1, one launch (start us, length us, event | category | flops | bytes accessed | tf_op | source)
XLA Modules:
  0.0 67.7 jit_solution(528307325580324515)
XLA Ops:
  0.0 1.3 %copy.11 = f32[2,36,4,720]{3,1,2,0:T(8,128)S(1)} copy(f32[2,36,4,720]{3,2,1,0:T(4,128)} %param.6) | data formatting | bytes 1658880 | tf_op args[0]
  1.4 0.0 copy-start.1
  1.4 0.0 copy-start
  1.4 0.0 copy-start.2
  1.4 0.0 copy-start.3
  1.4 0.0 copy-start.4
  1.5 1.2 %fusion.x_ref = f32[2,4,48,768]{3,2,1,0:T(8,128)} fusion(f32[2,4,4,720]{3,2,1,0:T(4,128)S(1)} %slice.33, f32[2,4,36,720]{3,2,1,0:T(8,128)S(1)} %bitcast.9, f32[2,4,8,720]{3,2,1,0:T(8,128)S(1)} %slice.32), kind=kLoop, calls=%fused_computation.3 | loop fusion | flops 5308416 | bytes 2285568 | tf_op jit(solution)/shard_map/concatenate | solution.py:360
  2.7 0.0 copy-done.1
  2.7 0.1 fusion.7
  2.8 0.0 copy-done
  2.8 0.1 fusion.8
  2.9 0.7 %pad_maximum_fusion.2 = (f32[4,768]{1,0:T(4,128)}, f32[4,768]{1,0:T(4,128)}) fusion(f32[4,24]{1,0:T(4,128)S(1)} %get-tuple-element.12, f32[4,24]{1,0:T(4,128)S(1)} %get-tuple-element.11, f32[4,720]{1,0:T(4,128)S(1)} %copy-done, f32[4,24]{1,0:T(4,128)S(1)} %get-tuple-element.10, f32[4,24]{1,0:T(4,128)S(1)} %get-tuple-element.9, f32[4,720]{1,0:T(4,128)S(1)} %copy-done.1), kind=kLoop, calls=%fused_computation.15 | loop fusion | flops 12288 | bytes 49152 | tf_op jit(solution)/shard_map/concatenate | solution.py:360
  3.5 0.0 copy-done.2
  3.6 0.0 copy-done.3
  3.7 0.0 copy-done.4
  3.7 0.6 pad_maximum_fusion.obs_ref
  4.3 0.7 %broadcast_in_dim.2.trig_ref = f32[2,36,128]{2,1,0:T(8,128)} broadcast(f32[2,36]{1,0:T(2,128)S(1)} %pad_maximum_fusion.4), dimensions={0,1} | broadcast | bytes 37152 | tf_op jit(solution)/shard_map/broadcast_in_dim | solution.py:366
  5.0 50.2 %propagate.1 = (f32[8,72,384]{2,1,0:T(8,128)}, f32[8,8,512]{2,1,0:T(8,128)}) custom-call(f32[2,4,48,768]{3,2,1,0:T(8,128)} %fusion.x_ref, f32[4,768]{1,0:T(4,128)} %get-tuple-element.17.speed_ref, f32[4,768]{1,0:T(4,128)} %get-tuple-element.18.turn_ref, f32[2,36,128]{2,1,0:T(8,128)} %broadcast_in_dim.2.trig_ref, f32[8,1024]{1,0:T(8,128)} %pad_maximum_fusion.obs_ref), custom_call_target="tpu_custom_call" | custom-call | tf_op jit(solution)/shard_map/propagate/pallas_call | solution.py:211
  55.2 10.2 %analyse.1 = f32[16,36,360]{2,1,0:T(8,128)} custom-call(f32[8,72,384]{2,1,0:T(8,128)} %get-tuple-element.7.state_ref, f32[8,8,512]{2,1,0:T(8,128)} %get-tuple-element.8.block_ref, f32[8,1024]{1,0:T(8,128)} %pad_maximum_fusion.obs_ref), custom_call_target="tpu_custom_call" | custom-call | tf_op jit(solution)/shard_map/analyse/pallas_call | solution.py:340
  65.4 2.3 %copy.9 = f32[16,36,360]{2,0,1:T(8,128)} copy(f32[16,36,360]{2,1,0:T(8,128)} %analyse.1) | data formatting | bytes 1658880 | tf_op jit(solution)/shard_map/analyse/pallas_call | solution.py:340
  (8 shorter events, 0.2 us)
Async XLA Ops:
  1.4 1.3 %copy-start.1 = (f32[4,720]{1,0:T(4,128)S(1)}, f32[4,720]{1,0:T(4,128)}, u32[]{:S(2)}) copy-start(f32[4,720]{1,0:T(4,128)} %param.8) | copy-start | bytes 34564
  1.4 1.4 %copy-start = (f32[4,720]{1,0:T(4,128)S(1)}, f32[4,720]{1,0:T(4,128)}, u32[]{:S(2)}) copy-start(f32[4,720]{1,0:T(4,128)} %param.7) | copy-start | bytes 34564
  1.4 2.1 %copy-start.2 = (s32[2,1024]{1,0:T(2,128)S(1)}, s32[2,1024]{1,0:T(2,128)}, u32[]{:S(2)}) copy-start(s32[2,1024]{1,0:T(2,128)} %param.9) | copy-start | bytes 24580
  1.4 2.2 %copy-start.3 = (f32[2,1024]{1,0:T(2,128)S(1)}, f32[2,1024]{1,0:T(2,128)}, u32[]{:S(2)}) copy-start(f32[2,1024]{1,0:T(2,128)} %param.11) | copy-start | bytes 24580
  1.4 2.2 %copy-start.4 = (f32[2,1024]{1,0:T(2,128)S(1)}, f32[2,1024]{1,0:T(2,128)}, u32[]{:S(2)}) copy-start(f32[2,1024]{1,0:T(2,128)} %param.10) | copy-start | bytes 24580

commit v2 on v0

v2 whole, which is shorter than its diff:
```python
import functools
import math

import jax
import jax.numpy as jnp
import numpy as np
from jax import lax
from jax.experimental import pallas as pl
from jax.experimental.pallas import tpu as pltpu
from jax.sharding import PartitionSpec as P

LON = 720
STEPS = 4
BATCHES = 2
LOC = 4
DIRS = 36
NOBS = 1024
MEMBERS = 16
ROWS = 4
OWN = 360
WIDE = 768
TALL = 48
BASE = 8
PART = 384
HALF = 24
CHUNK = 512
F32 = jnp.float32
BF16 = jnp.bfloat16


def step_row(centre, behind, ahead, upwind_y, cx, cy, cr, pick_x):
    west = pltpu.roll(centre, 1, axis=1)
    east = pltpu.roll(centre, WIDE - 1, axis=1)
    result = centre - cx * (centre - jnp.where(pick_x, west, east))
    result = result - cy * (centre - upwind_y)
    return result - jnp.abs(cr) * (centre - jnp.where(cr > 0.0, behind, ahead))


def widen(array):
    return jnp.concatenate([array, array[:, :24], array[:, LON - 24:]], axis=1)


def panel(prior, values, variance):
    centre = jnp.sum(prior, axis=0, keepdims=True) * (1.0 / MEMBERS)
    anomaly = prior - centre
    spread = jnp.sum(anomaly * anomaly, axis=0, keepdims=True) * (1.0 / (MEMBERS - 1))
    total = spread + variance
    shrink = 1.0 / (1.0 + jnp.sqrt(variance / total))
    coef = ((values - centre) - shrink * anomaly) / (total * (MEMBERS - 1))
    return anomaly, coef


def split_mix(anomaly, coef, high_ref, low_ref):
    for l in range(MEMBERS):
        mix = anomaly * coef[l:l + 1]
        high = mix.astype(BF16)
        high_ref[l * MEMBERS:(l + 1) * MEMBERS, :] = high
        low_ref[l * MEMBERS:(l + 1) * MEMBERS, :] = (mix - high.astype(F32)).astype(BF16)


def taper(row, lon, rows, lons):
    lat_gap = row - rows
    lon_gap = jnp.abs(lon - lons)
    lon_gap = jnp.minimum(lon_gap, LON - lon_gap)
    near = jnp.maximum(1.0 - (lat_gap * lat_gap + lon_gap * lon_gap) * (1.0 / (LOC * LOC)), 0.0)
    return (near * near).astype(BF16)


def mixed(high_ref, low_ref, weights):
    dims = (((1,), (1,)), ((), ()))
    return lax.dot_general(
        high_ref[...], weights, dims, preferred_element_type=F32
    ) + lax.dot_general(low_ref[...], weights, dims, preferred_element_type=F32)


def wave_kernel(
    spaces, peers,
    x_ref, speed_ref, turn_ref, trig_ref, cell_ref, value_ref, variance_ref,
    out_ref,
    e_ref, south_ref, north_ref, cx_ref, cy_ref, cr_ref, send_ref, mean_ref,
    mine_ref, near_ref, sum_ref, state_ref, block_ref, place_ref, column_ref,
    cross_ref, taper_ref, onehot_ref, s_ref, prior_ref, next_ref,
    high_ref, low_ref, gain_ref, total_ref,
    halo_send, halo_recv, part_send, part_recv, near_send, near_recv,
    all_send, all_recv, own_sem,
):
    space = lax.axis_index("space")
    member = lax.axis_index("member")
    shifts = (1, spaces - 1, 2, spaces - 2)

    barrier = pltpu.get_barrier_semaphore()
    for shift in shifts:
        pl.semaphore_signal(
            barrier, inc=1, device_id=(lax.rem(space + shift, spaces), member),
            device_id_type=pl.DeviceIdType.MESH)
    for offset in range(1, peers):
        pl.semaphore_signal(
            barrier, inc=1, device_id=(space, lax.rem(member + offset, peers)),
            device_id_type=pl.DeviceIdType.MESH)

    def keep(step, m, r, new):
        e_ref[step, m, r, BASE:BASE + DIRS, :] = new
        e_ref[step, m, r, BASE - 1:BASE, :] = new[DIRS - 1:DIRS]
        e_ref[step, m, r, BASE + DIRS:BASE + DIRS + 1, :] = new[0:1]

    for r in (0, ROWS - 1, 1, 2):
        for m in range(2):
            keep(0, m, r, widen(x_ref[m, r]))
    pl.semaphore_wait(barrier, len(shifts) + peers - 1)

    def halo(step, m, side):
        if side == 0:
            source = e_ref.at[step, m, ROWS - 1, pl.ds(BASE, HALF)]
            target, to = south_ref.at[step, m], lax.rem(space + 1, spaces)
        else:
            source = e_ref.at[step, m, 0, pl.ds(BASE + 16, HALF)]
            target, to = north_ref.at[step, m], lax.rem(space + spaces - 1, spaces)
        return pltpu.make_async_remote_copy(
            src_ref=source, dst_ref=target,
            send_sem=halo_send.at[step, m, side], recv_sem=halo_recv.at[step, m, side],
            device_id=(to, member), device_id_type=pl.DeviceIdType.MESH)

    for m in range(2):
        for side in range(2):
            halo(0, m, side).start()

    cosines = jnp.concatenate([trig_ref[0]] * (WIDE // 128), axis=1)
    sines = jnp.concatenate([trig_ref[1]] * (WIDE // 128), axis=1)
    speeds = widen(speed_ref[...])
    turns = widen(turn_ref[...])
    for r in range(ROWS):
        cx_ref[r] = speeds[r:r + 1, :] * jnp.abs(cosines)
        cy_ref[r] = speeds[r:r + 1, :] * jnp.abs(sines)
        cr_ref[r] = turns[r:r + 1, :] * cosines
    pick_x = cosines > 0.0
    pick_y = sines > 0.0
    has_south = (space > 0).astype(F32)
    has_north = (space < spaces - 1).astype(F32)

    cells = cell_ref[...].astype(F32)
    rows = jnp.floor((cells + 0.5) * (1.0 / LON))
    lons = cells - rows * float(LON)
    place_ref[...] = jnp.concatenate([rows, lons, rows, lons], axis=0)
    column_ref[...] = jnp.transpose(place_ref[...])

    device = space * peers + member
    own_row = (device // 2).astype(F32)
    own_lon = ((device % 2) * OWN).astype(F32)

    def own_taper(batch):
        cell_lon = lax.broadcasted_iota(jnp.int32, (PART, 128), 0).astype(F32) + own_lon
        cell_lon = jnp.concatenate([cell_lon] * (NOBS // 128), axis=1)
        taper_ref[batch] = taper(own_row, cell_lon, place_ref[batch:batch + 1, :],
                                 place_ref[2 + batch:3 + batch, :])

    width = 256

    def cross_taper(at):
        cross_ref[at:at + width, :] = taper(
            column_ref[at:at + width, 1:2], column_ref[at:at + width, 3:4],
            place_ref[0:1, :], place_ref[2:3, :])

    def select(chunk):
        batch, part_of = divmod(chunk, NOBS // CHUNK)
        lanes = slice(part_of * CHUNK, (part_of + 1) * CHUNK)
        where_lon = lax.broadcasted_iota(jnp.int32, (WIDE, CHUNK), 0).astype(F32)
        onehot_ref[chunk] = jnp.where(
            where_lon == place_ref[2 + batch:3 + batch, lanes], 1.0, 0.0).astype(BF16)

    filler = {
        (0, 0): [lambda: own_taper(0)],
        (0, 1): [lambda: own_taper(1)],
        (1, 0): [lambda: cross_taper(0)],
        (1, 1): [lambda: cross_taper(width)],
        (2, 0): [lambda: cross_taper(2 * width)],
        (2, 1): [lambda: cross_taper(3 * width)],
        (3, 0): [lambda: select(0), lambda: select(1)],
        (3, 1): [lambda: select(2), lambda: select(3)],
    }

    def advance(step, m, r):
        centre = e_ref[step, m, r, BASE:BASE + DIRS, :]
        behind = e_ref[step, m, r, BASE - 1:BASE - 1 + DIRS, :]
        ahead = e_ref[step, m, r, BASE + 1:BASE + 1 + DIRS, :]
        if r > 0:
            south = e_ref[step, m, r - 1, BASE:BASE + DIRS, :]
        if r < ROWS - 1:
            north = e_ref[step, m, r + 1, BASE:BASE + DIRS, :]
        if r == 0:
            south = jnp.concatenate([south_ref[step, m] * has_south, north[HALF:]], axis=0)
        if r == ROWS - 1:
            north = jnp.concatenate(
                [south[:16], (north_ref[step, m] * has_north)[:DIRS - 16]], axis=0)
        new = step_row(centre, behind, ahead, jnp.where(pick_y, south, north),
                       cx_ref[r], cy_ref[r], cr_ref[r], pick_x)
        if step < STEPS - 1:
            keep(step + 1, m, r, new)
        else:
            mean_ref[m * ROWS + r:m * ROWS + r + 1, :] = (
                jnp.sum(new, axis=0, keepdims=True) * (1.0 / DIRS))
            send_ref[2 * r, m * DIRS:(m + 1) * DIRS, :] = new[:, :PART]
            send_ref[2 * r + 1, m * DIRS:(m + 1) * DIRS, :] = pltpu.roll(
                new, WIDE - OWN, axis=1)[:, :PART]

    cuts = ((0, 32), (32, 40))

    def part(m, offset):
        to = lax.rem(member + offset, peers)
        first, count = cuts[m]
        return pltpu.make_async_remote_copy(
            src_ref=send_ref.at[to, pl.ds(first, count)],
            dst_ref=state_ref.at[member, pl.ds(first, count)],
            send_sem=part_send.at[m, offset], recv_sem=part_recv.at[m, offset],
            device_id=(space, to), device_id_type=pl.DeviceIdType.MESH)

    order = (4, 3, 5, 2, 6, 1, 7)
    for step in range(STEPS):
        for m in range(2):
            for r in range(1, ROWS - 1):
                advance(step, m, r)
            for work in filler[(step, m)]:
                work()
            halo(step, m, 0).wait_recv()
            advance(step, m, 0)
            if step < STEPS - 1:
                halo(step + 1, m, 1).start()
            halo(step, m, 1).wait_recv()
            advance(step, m, ROWS - 1)
            if step < STEPS - 1:
                halo(step + 1, m, 0).start()
            elif m == 0:
                for offset in order:
                    part(0, offset).start()

    mean = mean_ref[...]
    high = mean.astype(BF16)
    rest = mean - high.astype(F32)
    middle = rest.astype(BF16)
    low = (rest - middle.astype(F32)).astype(BF16)
    slab = (space * ROWS).astype(F32)
    for chunk in range(BATCHES * NOBS // CHUNK):
        batch, part_of = divmod(chunk, NOBS // CHUNK)
        lanes = slice(part_of * CHUNK, (part_of + 1) * CHUNK)
        onehot = onehot_ref[chunk]
        found = (
            jnp.dot(high, onehot, preferred_element_type=F32)
            + jnp.dot(middle, onehot, preferred_element_type=F32)
            + jnp.dot(low, onehot, preferred_element_type=F32))
        row = place_ref[batch:batch + 1, lanes] - slab
        for m in range(2):
            value = jnp.zeros((1, CHUNK), F32)
            for r in range(ROWS):
                value = value + jnp.where(row == float(r), found[m * ROWS + r:m * ROWS + r + 1], 0.0)
            mine_ref[m * 4 + chunk:m * 4 + chunk + 1, :] = value

    def near(index):
        return pltpu.make_async_remote_copy(
            src_ref=mine_ref, dst_ref=near_ref.at[index],
            send_sem=near_send.at[index], recv_sem=near_recv.at[index],
            device_id=(lax.rem(space + shifts[index], spaces), member),
            device_id_type=pl.DeviceIdType.MESH)

    for index in range(4):
        near(index).start()
    own = pltpu.make_async_copy(send_ref.at[member], state_ref.at[member], own_sem)
    own.start()
    for index in range(4):
        near(index).wait_recv()
    sum_ref[...] = mine_ref[...] + near_ref[0] + near_ref[1] + near_ref[2] + near_ref[3]
    block_ref[member] = sum_ref[...]

    def everyone(offset):
        return pltpu.make_async_remote_copy(
            src_ref=sum_ref, dst_ref=block_ref.at[member],
            send_sem=all_send.at[offset], recv_sem=all_recv.at[offset],
            device_id=(space, lax.rem(member + offset, peers)),
            device_id_type=pl.DeviceIdType.MESH)

    for offset in order:
        everyone(offset).start()
    for offset in order:
        part(1, offset).start()
    for offset in order:
        everyone(offset).wait_recv()

    for k in range(MEMBERS):
        for chunk in range(4):
            at = (k % 2) * 4 + chunk
            prior_ref[k:k + 1, chunk * CHUNK:(chunk + 1) * CHUNK] = block_ref[k // 2, at:at + 1, :]
    anomaly, coef = panel(prior_ref[:, :NOBS], value_ref[0:1, :], variance_ref[0:1, :])
    split_mix(anomaly, coef, high_ref, low_ref)
    for at in range(0, NOBS, width):
        gain = mixed(high_ref, low_ref, cross_ref[at:at + width, :])
        prior = prior_ref[:, NOBS + at:NOBS + at + width]
        deviation = prior - jnp.sum(prior, axis=0, keepdims=True) * (1.0 / MEMBERS)
        for l in range(MEMBERS):
            next_ref[l:l + 1, at:at + width] = prior[l:l + 1] + jnp.sum(
                deviation * gain[l * MEMBERS:(l + 1) * MEMBERS], axis=0, keepdims=True)
    gain_ref[0] = mixed(high_ref, low_ref, taper_ref[0]).reshape(MEMBERS, MEMBERS, PART)
    anomaly, coef = panel(next_ref[...], value_ref[1:2, :], variance_ref[1:2, :])
    split_mix(anomaly, coef, high_ref, low_ref)
    gain_ref[1] = mixed(high_ref, low_ref, taper_ref[1]).reshape(MEMBERS, MEMBERS, PART)
    middle_gain = gain_ref[0, 0]
    for l in range(1, MEMBERS):
        middle_gain = middle_gain + gain_ref[0, l]
    middle_gain = middle_gain * (1.0 / MEMBERS)

    def compose(l, carry):
        later = gain_ref[1, l]
        total = gain_ref[0, l] + later
        for k in range(MEMBERS):
            total = total + (gain_ref[0, k] - middle_gain) * later[k:k + 1]
        total_ref[l] = total
        return carry

    lax.fori_loop(0, MEMBERS, compose, 0)

    for step in range(STEPS):
        for m in range(2):
            for side in range(2):
                halo(step, m, side).wait_send()
    own.wait()
    for index in range(4):
        near(index).wait_send()
    for offset in order:
        everyone(offset).wait_send()
    for m in range(2):
        for offset in order:
            part(m, offset).wait()

    for k in range(MEMBERS):
        first = (k % 2) * DIRS
        s_ref[k] = state_ref[k // 2, first:first + DIRS, :]
    centre = s_ref[0]
    for k in range(1, MEMBERS):
        centre = centre + s_ref[k]
    centre = centre * (1.0 / MEMBERS)
    for k in range(MEMBERS):
        s_ref[k] = s_ref[k] - centre
    mean_state = e_ref.at[0, 0, 0, pl.ds(0, DIRS), pl.ds(0, PART)]
    mean_state[...] = centre

    def update(l, carry):
        for tile in range(PART // 128):
            lanes = slice(tile * 128, (tile + 1) * 128)
            total = s_ref[l, :, lanes] + e_ref[0, 0, 0, 0:DIRS, lanes]
            gain = total_ref[l, :, lanes]
            for k in range(MEMBERS):
                total = total + s_ref[k, :, lanes] * gain[k:k + 1]
            count = min(128, OWN - tile * 128)
            out_ref[l, :, tile * 128:tile * 128 + count] = total[:, :count]
        return carry

    lax.fori_loop(0, MEMBERS, update, 0)


def fused(x, speed, turn, trig, cells, values, variances, spaces, peers):
    vmem = pl.BlockSpec(memory_space=pltpu.VMEM)
    dma = pltpu.SemaphoreType.DMA
    return pl.pallas_call(
        functools.partial(wave_kernel, spaces, peers),
        out_shape=jax.ShapeDtypeStruct((MEMBERS, DIRS, OWN), F32),
        in_specs=[vmem] * 7,
        out_specs=vmem,
        scratch_shapes=[
            pltpu.VMEM((STEPS, 2, ROWS, TALL, WIDE), F32),
            pltpu.VMEM((STEPS, 2, HALF, WIDE), F32),
            pltpu.VMEM((STEPS, 2, HALF, WIDE), F32),
            pltpu.VMEM((ROWS, DIRS, WIDE), F32),
            pltpu.VMEM((ROWS, DIRS, WIDE), F32),
            pltpu.VMEM((ROWS, DIRS, WIDE), F32),
            pltpu.VMEM((2 * ROWS, 2 * DIRS, PART), F32),
            pltpu.VMEM((2 * ROWS, WIDE), F32),
            pltpu.VMEM((8, CHUNK), F32),
            pltpu.VMEM((4, 8, CHUNK), F32),
            pltpu.VMEM((8, CHUNK), F32),
            pltpu.VMEM((peers, 2 * DIRS, PART), F32),
            pltpu.VMEM((peers, 8, CHUNK), F32),
            pltpu.VMEM((8, NOBS), F32),
            pltpu.VMEM((NOBS, 8), F32),
            pltpu.VMEM((NOBS, NOBS), BF16),
            pltpu.VMEM((BATCHES, PART, NOBS), BF16),
            pltpu.VMEM((BATCHES * NOBS // CHUNK, WIDE, CHUNK), BF16),
            pltpu.VMEM((MEMBERS, DIRS, PART), F32),
            pltpu.VMEM((MEMBERS, BATCHES * NOBS), F32),
            pltpu.VMEM((MEMBERS, NOBS), F32),
            pltpu.VMEM((MEMBERS * MEMBERS, NOBS), BF16),
            pltpu.VMEM((MEMBERS * MEMBERS, NOBS), BF16),
            pltpu.VMEM((BATCHES, MEMBERS, MEMBERS, PART), F32),
            pltpu.VMEM((MEMBERS, MEMBERS, PART), F32),
            dma((STEPS, 2, 2)), dma((STEPS, 2, 2)),
            dma((2, 8)), dma((2, 8)),
            dma((4,)), dma((4,)),
            dma((8,)), dma((8,)),
            dma(()),
        ],
        compiler_params=pltpu.CompilerParams(collective_id=0, has_side_effects=True),
        name="fused",
    )(x, speed, turn, trig, cells, values, variances)


def per_device(spectra, group_speed, turning_rate, obs_cell, obs_value, obs_variance):
    spaces, peers = lax.axis_size("space"), lax.axis_size("member")
    angles = (2.0 * math.pi * np.arange(DIRS, dtype=np.float32) / DIRS).astype(np.float32)
    trig = np.stack([np.cos(angles), np.sin(angles)]).astype(np.float32)
    trig = np.ascontiguousarray(np.broadcast_to(trig[:, :, None], (2, DIRS, 128)))
    x = jnp.transpose(spectra, (0, 2, 1, 3))
    return fused(x, group_speed, turning_rate, jnp.asarray(trig), obs_cell, obs_value,
                 obs_variance, spaces, peers)


def solution(mesh):
    placed = (P("member", None, "space", None), P("space", None), P("space", None), P(), P(), P())
    return jax.shard_map(
        per_device,
        mesh=mesh,
        in_specs=placed,
        out_specs=P(None, None, ("space", "member")),
        check_vma=False,
    )
```

time: 195 us -> 60 us (0.31)
  the two profiles are of different devices: /device:TPU:102 before, /device:TPU:1 now
where the time goes in v2:
time: 60 us; the launch traced here: 59.8 us
  Pallas kernels  55.2 us (92%)
  local copies, waits for them, and re-layouts  4.58 us (8%)
    pallas_call x1, Pallas kernels, fused(): pl.pallas_call(functools.partial(wave_kernel, spaces, peers), out_shape=j...  55.2 us
    unnamed x1, local copies, waits for them, and re-layouts  2.29 us
    pallas_call x1, local copies, waits for them, and re-layouts, fused(): pl.pallas_call(functools.partial(wave_kernel, spaces, peers), out_shape=j...  2.29 us

profile of v2, /device:TPU:1, one launch (start us, length us, event | category | flops | bytes accessed | tf_op | source)
XLA Modules:
  0.0 59.8 jit_solution(15756505476154029245)
XLA Ops:
  0.0 2.3 %copy.11 = f32[2,36,4,720]{3,1,2,0:T(8,128)} copy(f32[2,36,4,720]{3,2,1,0:T(4,128)} %param.7) | data formatting | bytes 1658880 | tf_op args[0]
  2.3 55.2 %fused.1 = f32[16,36,360]{2,1,0:T(8,128)} custom-call(f32[2,4,36,720]{3,2,1,0:T(8,128)} %bitcast.3, f32[4,720]{1,0:T(4,128)} %speed_ref.1, f32[4,720]{1,0:T(4,128)} %turn_ref.1, f32[2,36,128]{2,1,0:T(8,128)} %constant.2.clone.trig_ref, s32[2,1024]{1,0:T(2,128)} %cell_ref.1, f32[2,1024]{1,0:T(2,128)} %value_ref.1, f32[2,1024]{1,0:T(2,128)} %variance_ref.1), custom_call_target="tpu_custom_call" | custom-call | tf_op jit(solution)/shard_map/fused/pallas_call | solution.py:360
  57.5 2.3 %copy.9 = f32[16,36,360]{2,0,1:T(8,128)} copy(f32[16,36,360]{2,1,0:T(8,128)} %fused.1) | data formatting | bytes 1658880 | tf_op jit(solution)/shard_map/fused/pallas_call | solution.py:360

commit v3 on v2

--- a/solution.py
+++ b/solution.py
@@ -82,7 +82,7 @@
     cross_ref, taper_ref, onehot_ref, s_ref, prior_ref, next_ref,
     high_ref, low_ref, gain_ref, total_ref,
     halo_send, halo_recv, part_send, part_recv, near_send, near_recv,
-    all_send, all_recv, own_sem,
+    all_send, all_recv, own_sem, relay_ref, relay_send, relay_recv,
 ):
     space = lax.axis_index("space")
     member = lax.axis_index("member")
@@ -105,7 +105,7 @@
 
     for r in (0, ROWS - 1, 1, 2):
         for m in range(2):
-            keep(0, m, r, widen(x_ref[m, r]))
+            keep(0, m, r, widen(x_ref[m, :, r, :]))
     pl.semaphore_wait(barrier, len(shifts) + peers - 1)
 
     def halo(step, m, side):
@@ -204,14 +204,51 @@
 
     cuts = ((0, 32), (32, 40))
 
-    def part(m, offset):
-        to = lax.rem(member + offset, peers)
+    chips = peers // 2
+    chip, core = member // 2, lax.rem(member, 2)
+
+    def peer(away, other):
+        return 2 * lax.rem(chip + away + chips, chips) + (lax.rem(core + 1, 2) if other else core)
+
+    def part(m, index):
+        away, other = divmod(index, 2)
+        to = peer(away, other)
         first, count = cuts[m]
         return pltpu.make_async_remote_copy(
             src_ref=send_ref.at[to, pl.ds(first, count)],
             dst_ref=state_ref.at[member, pl.ds(first, count)],
-            send_sem=part_send.at[m, offset], recv_sem=part_recv.at[m, offset],
+            send_sem=part_send.at[m, index], recv_sem=part_recv.at[m, index],
             device_id=(space, to), device_id_type=pl.DeviceIdType.MESH)
+
+    def relay(m, other):
+        first, count = cuts[m]
+        return pltpu.make_async_remote_copy(
+            src_ref=send_ref.at[peer(2, other), pl.ds(first, count)],
+            dst_ref=relay_ref.at[m, other, pl.ds(0, count)],
+            send_sem=relay_send.at[m, other], recv_sem=relay_recv.at[m, other],
+            device_id=(space, peer(-1 if other else 1, False)),
+            device_id_type=pl.DeviceIdType.MESH)
+
+    def forward(m, other):
+        first, count = cuts[m]
+        step = -1 if other else 1
+        return pltpu.make_async_remote_copy(
+            src_ref=relay_ref.at[m, other, pl.ds(0, count)],
+            dst_ref=state_ref.at[peer(-step, False), pl.ds(first, count)],
+            send_sem=part_send.at[m, 4 + other], recv_sem=part_recv.at[m, 4 + other],
+            device_id=(space, peer(step, other)),
+            device_id_type=pl.DeviceIdType.MESH)
+
+    def scatter(m):
+        for other in range(2):
+            relay(m, other).start()
+        for index in (2, 6, 3, 7, 1):
+            part(m, index).start()
+
+    def pass_on(m):
+        for other in range(2):
+            relay(m, other).wait_recv()
+            forward(m, other).start()
 
     order = (4, 3, 5, 2, 6, 1, 7)
     for step in range(STEPS):
@@ -229,8 +266,7 @@
             if step < STEPS - 1:
                 halo(step + 1, m, 0).start()
             elif m == 0:
-                for offset in order:
-                    part(0, offset).start()
+                scatter(0)
 
     mean = mean_ref[...]
     high = mean.astype(BF16)
@@ -278,10 +314,11 @@
 
     for offset in order:
         everyone(offset).start()
-    for offset in order:
-        part(1, offset).start()
+    pass_on(0)
+    scatter(1)
     for offset in order:
         everyone(offset).wait_recv()
+    pass_on(1)
 
     for k in range(MEMBERS):
         for chunk in range(4):
@@ -325,8 +362,11 @@
     for offset in order:
         everyone(offset).wait_send()
     for m in range(2):
-        for offset in order:
-            part(m, offset).wait()
+        for index in (1, 2, 3, 6, 7):
+            part(m, index).wait()
+        for other in range(2):
+            relay(m, other).wait_send()
+            forward(m, other).wait()
 
     for k in range(MEMBERS):
         first = (k % 2) * DIRS
@@ -393,6 +433,8 @@
             dma((4,)), dma((4,)),
             dma((8,)), dma((8,)),
             dma(()),
+            pltpu.VMEM((2, 2, 40, PART), F32),
+            dma((2, 2)), dma((2, 2)),
         ],
         compiler_params=pltpu.CompilerParams(collective_id=0, has_side_effects=True),
         name="fused",
@@ -404,8 +446,7 @@
     angles = (2.0 * math.pi * np.arange(DIRS, dtype=np.float32) / DIRS).astype(np.float32)
     trig = np.stack([np.cos(angles), np.sin(angles)]).astype(np.float32)
     trig = np.ascontiguousarray(np.broadcast_to(trig[:, :, None], (2, DIRS, 128)))
-    x = jnp.transpose(spectra, (0, 2, 1, 3))
-    return fused(x, group_speed, turning_rate, jnp.asarray(trig), obs_cell, obs_value,
+    return fused(spectra, group_speed, turning_rate, jnp.asarray(trig), obs_cell, obs_value,
                  obs_variance, spaces, peers)
 
 

time: 60 us -> 58.7 us (0.978)
  local copies, waits for them, and re-layouts: 4.58 us -> 2.29 us
  Pallas kernels: 55.2 us -> 56.2 us
    unnamed x1 -> x0, local copies, waits for them, and re-layouts: 2.29 us -> none
    pallas_call x1, Pallas kernels: 55.2 us -> 56.2 us  [fused(): pl.pallas_call(functools.partial(wave_kernel, spaces, peers), out_shape=j...]
where the time goes in v3:
time: 58.7 us; the launch traced here: 58.5 us
  Pallas kernels  56.2 us (96%)
  local copies, waits for them, and re-layouts  2.29 us (4%)
    pallas_call x1, Pallas kernels, fused(): pl.pallas_call(functools.partial(wave_kernel, spaces, peers), out_shape=j...  56.2 us
    pallas_call x1, local copies, waits for them, and re-layouts, fused(): pl.pallas_call(functools.partial(wave_kernel, spaces, peers), out_shape=j...  2.29 us

profile of v3, /device:TPU:1, one launch (start us, length us, event | category | flops | bytes accessed | tf_op | source)
XLA Modules:
  0.0 58.5 jit_solution(17972459599522927100)
XLA Ops:
  0.0 56.2 %fused.1 = f32[16,36,360]{2,1,0:T(8,128)} custom-call(f32[2,36,4,720]{3,2,1,0:T(4,128)} %x_ref.1, f32[4,720]{1,0:T(4,128)} %speed_ref.1, f32[4,720]{1,0:T(4,128)} %turn_ref.1, f32[2,36,128]{2,1,0:T(8,128)} %constant.2.clone.trig_ref, s32[2,1024]{1,0:T(2,128)} %cell_ref.1, f32[2,1024]{1,0:T(2,128)} %value_ref.1, f32[2,1024]{1,0:T(2,128)} %variance_ref.1), custom_call_target="tpu_custom_call" | custom-call | tf_op jit(solution)/shard_map/fused/pallas_call | solution.py:400
  56.2 2.3 %copy.8 = f32[16,36,360]{2,0,1:T(8,128)} copy(f32[16,36,360]{2,1,0:T(8,128)} %fused.1) | data formatting | bytes 1658880 | tf_op jit(solution)/shard_map/fused/pallas_call | solution.py:400

commit v4 on v2

--- a/solution.py
+++ b/solution.py
@@ -105,7 +105,7 @@
 
     for r in (0, ROWS - 1, 1, 2):
         for m in range(2):
-            keep(0, m, r, widen(x_ref[m, r]))
+            keep(0, m, r, widen(x_ref[m, :, r, :]))
     pl.semaphore_wait(barrier, len(shifts) + peers - 1)
 
     def halo(step, m, side):
@@ -340,7 +340,7 @@
     mean_state = e_ref.at[0, 0, 0, pl.ds(0, DIRS), pl.ds(0, PART)]
     mean_state[...] = centre
 
-    def update(l, carry):
+    for l in range(MEMBERS):
         for tile in range(PART // 128):
             lanes = slice(tile * 128, (tile + 1) * 128)
             total = s_ref[l, :, lanes] + e_ref[0, 0, 0, 0:DIRS, lanes]
@@ -348,10 +348,7 @@
             for k in range(MEMBERS):
                 total = total + s_ref[k, :, lanes] * gain[k:k + 1]
             count = min(128, OWN - tile * 128)
-            out_ref[l, :, tile * 128:tile * 128 + count] = total[:, :count]
-        return carry
-
-    lax.fori_loop(0, MEMBERS, update, 0)
+            out_ref[:, l, tile * 128:tile * 128 + count] = total[:, :count]
 
 
 def fused(x, speed, turn, trig, cells, values, variances, spaces, peers):
@@ -359,7 +356,7 @@
     dma = pltpu.SemaphoreType.DMA
     return pl.pallas_call(
         functools.partial(wave_kernel, spaces, peers),
-        out_shape=jax.ShapeDtypeStruct((MEMBERS, DIRS, OWN), F32),
+        out_shape=jax.ShapeDtypeStruct((DIRS, MEMBERS, OWN), F32),
         in_specs=[vmem] * 7,
         out_specs=vmem,
         scratch_shapes=[
@@ -404,9 +401,9 @@
     angles = (2.0 * math.pi * np.arange(DIRS, dtype=np.float32) / DIRS).astype(np.float32)
     trig = np.stack([np.cos(angles), np.sin(angles)]).astype(np.float32)
     trig = np.ascontiguousarray(np.broadcast_to(trig[:, :, None], (2, DIRS, 128)))
-    x = jnp.transpose(spectra, (0, 2, 1, 3))
-    return fused(x, group_speed, turning_rate, jnp.asarray(trig), obs_cell, obs_value,
-                 obs_variance, spaces, peers)
+    analysis = fused(spectra, group_speed, turning_rate, jnp.asarray(trig), obs_cell, obs_value,
+                     obs_variance, spaces, peers)
+    return jnp.transpose(analysis, (1, 0, 2))
 
 
 def solution(mesh):

time: 60 us -> 57.7 us (0.962)
  local copies, waits for them, and re-layouts: 4.58 us -> 2.14 us
    pallas_call x1 -> x0, local copies, waits for them, and re-layouts: 2.29 us -> none  [fused(): pl.pallas_call(functools.partial(wave_kernel, spaces, peers), out_shape=j...]
where the time goes in v4:
time: 57.7 us; the launch traced here: 57.5 us
  Pallas kernels  55.4 us (96%)
  local copies, waits for them, and re-layouts  2.14 us (4%)
    pallas_call x1, Pallas kernels, fused(): pl.pallas_call(functools.partial(wave_kernel, spaces, peers), out_shape=j...  55.4 us
    unnamed x1, local copies, waits for them, and re-layouts  2.14 us

profile of v4, /device:TPU:1, one launch (start us, length us, event | category | flops | bytes accessed | tf_op | source)
XLA Modules:
  0.0 57.5 jit_solution(304484218492864871)
XLA Ops:
  0.0 55.4 %fused.1 = f32[36,16,360]{2,1,0:T(8,128)} custom-call(f32[2,36,4,720]{3,2,1,0:T(4,128)} %x_ref.1, f32[4,720]{1,0:T(4,128)} %speed_ref.1, f32[4,720]{1,0:T(4,128)} %turn_ref.1, f32[2,36,128]{2,1,0:T(8,128)} %constant.2.clone.trig_ref, s32[2,1024]{1,0:T(2,128)} %cell_ref.1, f32[2,1024]{1,0:T(2,128)} %value_ref.1, f32[2,1024]{1,0:T(2,128)} %variance_ref.1), custom_call_target="tpu_custom_call" | custom-call | tf_op jit(solution)/shard_map/fused/pallas_call | solution.py:357
  55.4 2.1 %copy.9 = f32[16,36,360]{2,0,1:T(8,128)} copy(f32[16,36,360]{2,0,1:T(8,128)} %bitcast.1) | data formatting | bytes 1658880

commit v5 on v4

--- a/solution.py
+++ b/solution.py
@@ -236,16 +236,15 @@
     high = mean.astype(BF16)
     rest = mean - high.astype(F32)
     middle = rest.astype(BF16)
-    low = (rest - middle.astype(F32)).astype(BF16)
+    low = rest - middle.astype(F32)
+    parts = jnp.concatenate([high.astype(F32), middle.astype(F32), low], axis=0).astype(BF16)
     slab = (space * ROWS).astype(F32)
     for chunk in range(BATCHES * NOBS // CHUNK):
         batch, part_of = divmod(chunk, NOBS // CHUNK)
         lanes = slice(part_of * CHUNK, (part_of + 1) * CHUNK)
         onehot = onehot_ref[chunk]
-        found = (
-            jnp.dot(high, onehot, preferred_element_type=F32)
-            + jnp.dot(middle, onehot, preferred_element_type=F32)
-            + jnp.dot(low, onehot, preferred_element_type=F32))
+        found = jnp.dot(parts, onehot, preferred_element_type=F32)
+        found = found[:8] + found[8:16] + found[16:]
         row = place_ref[batch:batch + 1, lanes] - slab
         for m in range(2):
             value = jnp.zeros((1, CHUNK), F32)

time: 57.7 us -> 57.1 us (0.990)
  Pallas kernels: 55.4 us -> 54.8 us
where the time goes in v5:
time: 57.1 us; the launch traced here: 57 us
  Pallas kernels  54.8 us (96%)
  local copies, waits for them, and re-layouts  2.14 us (4%)
    pallas_call x1, Pallas kernels, fused(): pl.pallas_call(functools.partial(wave_kernel, spaces, peers), out_shape=j...  54.8 us
    unnamed x1, local copies, waits for them, and re-layouts  2.14 us

profile of v5, /device:TPU:1, one launch (start us, length us, event | category | flops | bytes accessed | tf_op | source)
XLA Modules:
  0.0 57.0 jit_solution(2668968516716798891)
XLA Ops:
  0.0 54.8 %fused.1 = f32[36,16,360]{2,1,0:T(8,128)} custom-call(f32[2,36,4,720]{3,2,1,0:T(4,128)} %x_ref.1, f32[4,720]{1,0:T(4,128)} %speed_ref.1, f32[4,720]{1,0:T(4,128)} %turn_ref.1, f32[2,36,128]{2,1,0:T(8,128)} %constant.2.clone.trig_ref, s32[2,1024]{1,0:T(2,128)} %cell_ref.1, f32[2,1024]{1,0:T(2,128)} %value_ref.1, f32[2,1024]{1,0:T(2,128)} %variance_ref.1), custom_call_target="tpu_custom_call" | custom-call | tf_op jit(solution)/shard_map/fused/pallas_call | solution.py:356
  54.8 2.1 %copy.9 = f32[16,36,360]{2,0,1:T(8,128)} copy(f32[16,36,360]{2,0,1:T(8,128)} %bitcast.1) | data formatting | bytes 1658880
